TPU v7x, 32 devices: a whole 2x2x4 slice. The times are simulated.
32 devices in a mesh: dp: 2 (over core), expert: 4 (over y, x), mp: 4 (over z).
Axes of the slice: x: 2, y: 2, z: 4, core: 2. Of those that a mesh axis runs over, the one named last changes fastest.
Arguments:
- tokens: bfloat16 [512, 3072], P(('dp', 'expert')), may hold values from -6 to 6
- w_router: float32 [3072, 4], replicated, may hold values from -0.109375 to 0.109375
- expert_ids: int32 [512, 2], P(('dp', 'expert')), may hold values from 0 to 3, all different within a row; in each aligned block of 64 rows (0 to 63, 64 to 127, ...) at most 64 rows name the same one
- partner: int32 [4], replicated, may hold values from 0 to 3, as said below
- gate_weight: bfloat16 [4, 3072, 8192], P('expert', None, ('dp', 'mp')), may hold values from -0.109375 to 0.109375
- up_weight: bfloat16 [4, 3072, 8192], P('expert', None, ('dp', 'mp')), may hold values from -0.109375 to 0.109375
- down_weight: bfloat16 [4, 8192, 3072], P('expert', ('dp', 'mp')), may hold values from -0.0625 to 0.0625
- grad_out: bfloat16 [512, 3072], P(('dp', 'expert')), may hold values from -1.5 to 1.5
Outputs:
- mixed: bfloat16 [512, 3072], P(('dp', 'expert'))
- grad_tokens: bfloat16 [512, 3072], P(('dp', 'expert'))
- grad_router: float32 [3072, 4], replicated
- grad_gate: bfloat16 [4, 3072, 8192], P('expert', None, ('dp', 'mp'))
- grad_up: bfloat16 [4, 3072, 8192], P('expert', None, ('dp', 'mp'))
- grad_down: bfloat16 [4, 8192, 3072], P('expert', ('dp', 'mp'))
Inputs may be any that keep to these rules, and one draw needn't show every extreme that they name: `expert_ids`: each token names two different experts. Within each aligned block of 64 tokens no expert is named by more than 64 tokens, and in every draw some block names some expert exactly 64 times. A matching of the experts: partner[partner[e]] = e and partner[e] != e for every expert e.
All inputs are finite; a program needn't handle non-finite values.
Results may differ from a plain program's by a relative error of at most 0.019.
Values may be sent and summed in bfloat16 or wider, within the bound.
No kernel may reach another device: no remote copies, remote signals or barrier semaphores. Data moves between devices by JAX's collectives and lax.ppermute only.
A program may use at most 128 MiB of HBM per device.

v0:
```python
import jax
import jax.numpy as jnp
from jax import lax
from jax.sharding import PartitionSpec as P

exact_mode = lax.Precision.HIGHEST


def local(tokens, w_router, expert_ids, partner, gate_weight, up_weight, down_weight, grad_out):
    tok_rows, features = tokens.shape
    experts = w_router.shape[1]
    hid_part = gate_weight.shape[2]
    dp_count = lax.axis_size("dp")
    exp_count = lax.axis_size("expert")
    slot_count = min(tok_rows, 4 * tok_rows // experts)
    keep_count = 3 * slot_count // 4
    slot_total = experts * slot_count
    block_rows = exp_count * slot_count
    floats = tokens.astype(jnp.float32)
    logits = jnp.dot(floats, w_router, precision=exact_mode)
    chosen = (expert_ids[:, :, None] == lax.iota(jnp.int32, experts)[None, None, :]).astype(
        jnp.int32
    )
    chosen_float = chosen.astype(jnp.float32)
    picked = jnp.sum(logits[:, None, :] * chosen_float, axis=2)
    share_one = jax.nn.sigmoid(picked[:, 0] - picked[:, 1])
    shares = jnp.stack([share_one, 1.0 - share_one], axis=1)
    flat_choice = chosen.reshape(2 * tok_rows, experts)
    earlier = jnp.cumsum(flat_choice, axis=0) - flat_choice
    arrival = jnp.sum(earlier * flat_choice, axis=1).reshape(tok_rows, 2)
    partner_of = jnp.sum(chosen * partner[None, None, :], axis=2)
    target = jnp.where(arrival < keep_count, expert_ids, partner_of)
    slot_index = target * slot_count + arrival
    placing = (slot_index[:, :, None] == lax.iota(jnp.int32, slot_total)[None, None, :]).astype(
        jnp.bfloat16
    )
    send_tokens = jnp.einsum("tks,td->sd", placing, tokens, preferred_element_type=jnp.float32)
    send_tokens = send_tokens.astype(jnp.bfloat16).reshape(experts, slot_count, features)
    scaled = (shares[:, :, None] * grad_out.astype(jnp.float32)[:, None, :]).astype(jnp.bfloat16)
    send_cot = jnp.einsum("tks,tkd->sd", placing, scaled, preferred_element_type=jnp.float32)
    send_cot = send_cot.astype(jnp.bfloat16).reshape(experts, slot_count, features)

    def spread(buffer):
        arrived = lax.all_to_all(buffer, "expert", split_axis=0, concat_axis=0, tiled=True)
        return lax.all_gather(arrived, "dp", axis=0, tiled=True)

    rows_in = spread(send_tokens).reshape(-1, features)
    pieces = 1

    def combine(partial_value):
        summed = lax.psum(
            partial_value.reshape(dp_count, block_rows, features).astype(jnp.bfloat16), ("dp", "mp")
        ).astype(jnp.float32)
        own_rows = lax.dynamic_index_in_dim(summed, lax.axis_index("dp"), 0, keepdims=False)
        own_rows = own_rows.astype(jnp.bfloat16).reshape(exp_count, slot_count, features)
        restored = lax.all_to_all(own_rows, "expert", split_axis=0, concat_axis=0, tiled=True)
        return restored.reshape(slot_total, features)

    w_gate = gate_weight[0]
    w_up = up_weight[0]
    w_down = down_weight[0]
    pre_gate = jnp.dot(rows_in, w_gate, preferred_element_type=jnp.float32)
    pre_up = jnp.dot(rows_in, w_up, preferred_element_type=jnp.float32)
    sigmoid_gate = jax.nn.sigmoid(pre_gate)
    swished = pre_gate * sigmoid_gate
    hidden = (swished * pre_up).astype(jnp.bfloat16)
    down_split = w_down.reshape(hid_part, pieces, features // pieces)
    forward_terms = jnp.einsum(
        "prf,fqd->pqrd",
        hidden.reshape(dp_count, block_rows, hid_part),
        down_split,
        preferred_element_type=jnp.float32,
    )
    expert_out = combine(forward_terms)
    back_rows = jnp.einsum("tks,sd->tkd", placing, expert_out, preferred_element_type=jnp.float32)
    mixed = (shares[:, 0, None] * back_rows[:, 0] + shares[:, 1, None] * back_rows[:, 1]).astype(
        jnp.bfloat16
    )
    falling = grad_out.astype(jnp.float32)
    dshare = jnp.sum(falling[:, None, :] * back_rows, axis=2)
    dlogit = shares[:, 0] * shares[:, 1] * (dshare[:, 0] - dshare[:, 1])
    grad_logits = (chosen_float[:, 0] - chosen_float[:, 1]) * dlogit[:, None]
    router_term = lax.dot_general(
        floats, grad_logits, (((0,), (0,)), ((), ())), precision=exact_mode
    )
    grad_router = lax.psum(router_term.astype(jnp.bfloat16), ("dp", "expert")).astype(jnp.float32)
    router_back = jnp.dot(grad_logits, w_router.T, precision=exact_mode)
    cot_in = spread(send_cot).reshape(-1, features)
    dhidden = jnp.einsum("rd,fd->rf", cot_in, w_down, preferred_element_type=jnp.float32)
    up_grad = (dhidden * swished).astype(jnp.bfloat16)
    gate_grad = (dhidden * pre_up * sigmoid_gate * (1.0 + pre_gate * (1.0 - sigmoid_gate))).astype(
        jnp.bfloat16
    )
    grad_down = jnp.einsum("rf,rd->fd", hidden, cot_in, preferred_element_type=jnp.float32).astype(
        jnp.bfloat16
    )[None]
    grad_gate = jnp.einsum(
        "rd,rf->df", rows_in, gate_grad, preferred_element_type=jnp.float32
    ).astype(jnp.bfloat16)[None]
    grad_up = jnp.einsum("rd,rf->df", rows_in, up_grad, preferred_element_type=jnp.float32).astype(
        jnp.bfloat16
    )[None]
    gate_split = w_gate.reshape(pieces, features // pieces, hid_part)
    up_split = w_up.reshape(pieces, features // pieces, hid_part)
    backward_terms = jnp.einsum(
        "prf,qdf->pqrd",
        gate_grad.reshape(dp_count, block_rows, hid_part),
        gate_split,
        preferred_element_type=jnp.float32,
    )
    backward_terms = backward_terms + jnp.einsum(
        "prf,qdf->pqrd",
        up_grad.reshape(dp_count, block_rows, hid_part),
        up_split,
        preferred_element_type=jnp.float32,
    )
    row_grads = combine(backward_terms)
    grad_rows = jnp.einsum("tks,sd->tkd", placing, row_grads, preferred_element_type=jnp.float32)
    grad_tokens = (router_back + grad_rows[:, 0] + grad_rows[:, 1]).astype(jnp.bfloat16)
    return (mixed, grad_tokens, grad_router, grad_gate, grad_up, grad_down)


def solution(mesh):
    in_specs = (
        P(("dp", "expert"), None),
        P(),
        P(("dp", "expert"), None),
        P(),
        P("expert", None, ("dp", "mp")),
        P("expert", None, ("dp", "mp")),
        P("expert", ("dp", "mp"), None),
        P(("dp", "expert"), None),
    )
    out_specs = (
        P(("dp", "expert"), None),
        P(("dp", "expert"), None),
        P(),
        P("expert", None, ("dp", "mp")),
        P("expert", None, ("dp", "mp")),
        P("expert", ("dp", "mp"), None),
    )
    return jax.shard_map(local, mesh=mesh, in_specs=in_specs, out_specs=out_specs, check_vma=False)
```

profile of v0, /device:TPU:1, one launch (start us, length us, event | category | flops | bytes accessed | tf_op | source)
XLA Modules:
  0.0 329.8 jit_solution(508223752091180420)
XLA Ops:
  8.2 1.2 fusion.42
  14.2 22.7 %all_to_all.20 = bf16[4,64,3072]{2,1,0:T(8,128)(2,1)} all-to-all(bf16[4,64,3072]{2,1,0:T(8,128)(2,1)S(1)} %bitcast.108), channel_id=1, replica_groups=mesh['dp'=2,'expert'=4,'mp'=4] {'expert'}, dimensions={0} | all-to-all | bytes 3145728 | tf_op jit(solution)/shard_map/all_to_all | solution.py:44
  37.6 20.3 %all_to_all.21 = bf16[4,64,3072]{2,1,0:T(8,128)(2,1)} all-to-all(bf16[4,64,3072]{2,1,0:T(8,128)(2,1)S(1)} %bitcast.105), channel_id=1, replica_groups=mesh['dp'=2,'expert'=4,'mp'=4] {'expert'}, dimensions={0} | all-to-all | bytes 3145728 | tf_op jit(solution)/shard_map/all_to_all | solution.py:44
  58.0 6.5 %fusion.6 = f32[512,1024]{1,0:T(8,128)S(1)} fusion(bf16[512,3072]{1,0:T(8,128)(2,1)} %bitcast.120, bf16[1,1024,3072]{2,1,0:T(8,128)(2,1)} %param.14), kind=kOutput, calls=%fused_computation.6 | convolution fusion | flops 3221225472 | bytes 11534336 | tf_op jit(solution)/shard_map/rd,fd->rf/dot_general | solution.py:89
  64.6 8.7 %all-gather.3.cloned.1.call-done = bf16[8,64,3072]{2,1,0:T(8,128)(2,1)} async-done(((bf16[4,64,3072]{2,1,0:T(8,128)(2,1)}), bf16[8,64,3072]{2,1,0:T(8,128)(2,1)}) %all-gather.3.cloned.1.call-update) | async-done | bytes 3145744 | tf_op jit(solution)/shard_map/all_gather | solution.py:45
  73.3 6.6 %fusion.8 = f32[512,1024]{1,0:T(8,128)S(1)} fusion(bf16[512,3072]{1,0:T(8,128)(2,1)} %bitcast.116, bf16[1,3072,1024]{2,1,0:T(8,128)(2,1)} %param.13), kind=kOutput, calls=%fused_computation.8 | convolution fusion | flops 3221225472 | bytes 11534336 | tf_op jit(solution)/shard_map/dot_general | solution.py:63
  79.9 7.3 %multiply_convert_fusion.1 = (bf16[512,1024]{1,0:T(8,128)(2,1)S(1)}, bf16[512,1024]{1,0:T(8,128)(2,1)S(1)}, bf16[512,1024]{1,0:T(8,128)(2,1)S(1)}) fusion(f32[512,1024]{1,0:T(8,128)S(1)} %fusion.6, f32[512,1024]{1,0:T(8,128)S(1)} %fusion.8, bf16[512,3072]{1,0:T(8,128)(2,1)S(1)} %bitcast.118, bf16[1,3072,1024]{2,1,0:T(8,128)(2,1)} %param.12), kind=kOutput, calls=%fused_computation.28 | convolution fusion | flops 3229089792 | bytes 16777216 | tf_op jit(solution)/shard_map/dot_general | solution.py:62
  87.3 5.4 %fusion = f32[2,256,3072]{2,1,0:T(8,128)} fusion(bf16[2,256,1024]{2,1,0:T(8,128)(2,1)S(1)} %bitcast.123, bf16[1,3072,1024]{2,1,0:T(8,128)(2,1)S(1)} %bitcast.111), kind=kOutput, calls=%fused_computation | convolution fusion | flops 3221225472 | bytes 13631488 | tf_op jit(solution)/shard_map/prf,qdf->pqrd/dot_general | solution.py:111
  92.7 4.8 %fusion.14 = bf16[2,256,3072]{2,1,0:T(8,128)(2,1)} fusion(bf16[2,256,1024]{2,1,0:T(8,128)(2,1)S(1)} %bitcast.124, bf16[1,1024,3072]{2,1,0:T(8,128)(2,1)S(1)} %bitcast.113), kind=kOutput, calls=%fused_computation.16 | convolution fusion | flops 3222798336 | bytes 10485760 | tf_op jit(solution)/shard_map/prf,fqd->pqrd/dot_general | solution.py:68
  97.5 6.8 %add_convert_fusion = bf16[2,256,3072]{2,1,0:T(8,128)(2,1)} fusion(f32[2,256,3072]{2,1,0:T(8,128)} %fusion, bf16[2,256,1024]{2,1,0:T(8,128)(2,1)S(1)} %bitcast.122, bf16[1,3072,1024]{2,1,0:T(8,128)(2,1)S(1)} %bitcast.115), kind=kOutput, calls=%fused_computation.15 | convolution fusion | flops 3224371200 | bytes 16777216 | tf_op jit(solution)/shard_map/prf,qdf->pqrd/dot_general | solution.py:105
  104.4 137.3 %all-reduce.3.cloned.1.call-done = (bf16[2,256,3072]{2,1,0:T(8,128)(2,1)}, bf16[2,256,3072]{2,1,0:T(8,128)(2,1)}) async-done(((bf16[2,256,3072]{2,1,0:T(8,128)(2,1)}, bf16[2,256,3072]{2,1,0:T(8,128)(2,1)}), (bf16[2,256,3072]{2,1,0:T(8,128)(2,1)}, bf16[2,256,3072]{2,1,0:T(8,128)(2,1)})) %all-reduce.3.cloned.1.call-update) | async-done | bytes 6291472 | tf_op jit(solution)/shard_map/psum | solution.py:51
  241.6 2.7 convert_convert_fusion
  244.3 3.7 %all-to-all-start.3 = ((bf16[4,64,3072]{2,1,0:T(8,128)(2,1)}), bf16[4,64,3072]{2,1,0:T(8,128)(2,1)S(1)}, u32[]{:S(2)}, u32[]{:S(2)}) async-start(bf16[4,64,3072]{2,1,0:T(8,128)(2,1)} %bitcast.107), calls=%async_computation.3 | async-start | bytes 3145728 | tf_op jit(solution)/shard_map/all_to_all | solution.py:56
  248.1 8.5 %convert_bitcast_fusion = bf16[1,1024,3072]{2,1,0:T(8,128)(2,1)} fusion(bf16[512,1024]{1,0:T(8,128)(2,1)} %copy-done.10, bf16[512,3072]{1,0:T(8,128)(2,1)} %bitcast.121), kind=kOutput, calls=%fused_computation.12 | convolution fusion | flops 3224371200 | bytes 10485760 | tf_op jit(solution)/shard_map/rf,rd->fd/dot_general | solution.py:94
  256.6 1.3 convert_convert_fusion.1
  257.9 8.6 %all-to-all-done.3 = bf16[4,64,3072]{2,1,0:T(8,128)(2,1)S(1)} async-done(((bf16[4,64,3072]{2,1,0:T(8,128)(2,1)}), bf16[4,64,3072]{2,1,0:T(8,128)(2,1)S(1)}, u32[]{:S(2)}, u32[]{:S(2)}) %all-to-all-start.3) | async-done | bytes 1572896 | tf_op jit(solution)/shard_map/all_to_all | solution.py:56
  266.6 4.4 %all-to-all-start.1 = ((bf16[4,64,3072]{2,1,0:T(8,128)(2,1)}), bf16[4,64,3072]{2,1,0:T(8,128)(2,1)}, u32[]{:S(2)}, u32[]{:S(2)}) async-start(bf16[4,64,3072]{2,1,0:T(8,128)(2,1)} %bitcast.106), calls=%async_computation.1 | async-start | bytes 3145728 | tf_op jit(solution)/shard_map/all_to_all | solution.py:56
  270.9 8.5 %convert_bitcast_fusion.1 = bf16[1,3072,1024]{2,1,0:T(8,128)(2,1)} fusion(bf16[512,3072]{1,0:T(8,128)(2,1)} %bitcast.117, bf16[512,1024]{1,0:T(8,128)(2,1)} %copy-done.9), kind=kOutput, calls=%fused_computation.13 | convolution fusion | flops 3224371200 | bytes 10485760 | tf_op jit(solution)/shard_map/rd,rf->df/dot_general | solution.py:100
  279.5 5.4 %convert_bitcast_fusion.2 = bf16[1,3072,1024]{2,1,0:T(8,128)(2,1)} fusion(bf16[512,3072]{1,0:T(8,128)(2,1)S(1)} %bitcast.119, bf16[512,1024]{1,0:T(8,128)(2,1)S(1)} %copy-done.8), kind=kOutput, calls=%fused_computation.14 | convolution fusion | flops 3224371200 | bytes 10485760 | tf_op jit(solution)/shard_map/rd,rf->df/dot_general | solution.py:97
  284.8 1.6 fusion.28
  286.4 3.3 all-to-all-done.1
  289.7 2.1 multiply_reduce_fusion
  292.0 1.6 fusion.19
  293.7 28.0 %psum.23 = bf16[3072,4]{0,1:T(4,128)(2,1)S(1)} all-reduce(bf16[3072,4]{0,1:T(4,128)(2,1)S(1)} %fusion.20), channel_id=1, replica_groups=mesh['dp'=2,'expert'=4,'mp'=4] {'dp','expert'}, use_global_device_ids=true, to_apply=%region_8.9 | all-reduce | flops 12288 | bytes 49152 | tf_op jit(solution)/shard_map/psum | solution.py:86
  (66 shorter events, 8.5 us)
Async XLA Ops:
  7.2 1.0 copy-start
  7.2 50.8 %all-gather.5.cloned.1.call-start = ((), (), s32[]{:S(2)}) async-start(), calls=%async_computation.5 | async-start | bytes 4718592 | tf_op jit(solution)/shard_map/all_gather | solution.py:45
  36.9 36.4 %all-gather.3.cloned.1.call-start = ((), (), s32[]{:S(2)}) async-start(), calls=%async_computation.4 | async-start | bytes 4718592 | tf_op jit(solution)/shard_map/all_gather | solution.py:45
  57.9 183.7 %all-reduce.3.cloned.1.call-start = ((), (), s32[]{:S(2)}) async-start(), calls=%async_computation.6 | async-start | bytes 12582912 | tf_op jit(solution)/shard_map/psum | solution.py:51
  73.3 6.6 %copy-start.5 = (bf16[8,64,3072]{2,1,0:T(8,128)(2,1)S(1)}, bf16[8,64,3072]{2,1,0:T(8,128)(2,1)}, u32[]{:S(2)}) copy-start(bf16[8,64,3072]{2,1,0:T(8,128)(2,1)} %all-gather.3.cloned.1.call-done) | copy-start | bytes 9437188
  73.3 14.0 %slice-start = ((s8[6291456]{0:T(1024)(128)(4,1)}), s8[4194304]{0:T(1024)(128)(4,1)S(1)}, s32[]{:S(2)}) async-start(s8[6291456]{0:T(1024)(128)(4,1)} %bitcast.110), calls=%async_computation.7 | async-start | bytes 8388608
  73.3 19.4 %slice-start.2 = ((s8[6291456]{0:T(1024)(128)(4,1)}), s8[4194304]{0:T(1024)(128)(4,1)S(1)}, s32[]{:S(2)}) async-start(s8[6291456]{0:T(1024)(128)(4,1)} %bitcast.112), calls=%async_computation.9 | async-start | bytes 8388608
  79.9 7.4 %slice-start.1 = ((s8[6291456]{0:T(1024)(128)(4,1)}), s8[2097152]{0:T(1024)(128)(4,1)S(1)}, s32[]{:S(2)}) async-start(s8[6291456]{0:T(1024)(128)(4,1)} %bitcast.110), calls=%async_computation.8 | async-start | bytes 4194304
  79.9 12.8 %slice-start.3 = ((s8[6291456]{0:T(1024)(128)(4,1)}), s8[2097152]{0:T(1024)(128)(4,1)S(1)}, s32[]{:S(2)}) async-start(s8[6291456]{0:T(1024)(128)(4,1)} %bitcast.112), calls=%async_computation.10 | async-start | bytes 4194304
  79.9 17.6 %slice-start.4 = ((s8[6291456]{0:T(1024)(128)(4,1)}), s8[4194304]{0:T(1024)(128)(4,1)S(1)}, s32[]{:S(2)}) async-start(s8[6291456]{0:T(1024)(128)(4,1)} %bitcast.114), calls=%async_computation.11 | async-start | bytes 8388608
  87.2 5.4 %copy-start.9 = (bf16[512,1024]{1,0:T(8,128)(2,1)}, bf16[512,1024]{1,0:T(8,128)(2,1)S(1)}, u32[]{:S(2)}) copy-start(bf16[512,1024]{1,0:T(8,128)(2,1)S(1)} %get-tuple-element.11) | copy-start | bytes 3145732
  87.2 5.4 %copy-start.10 = (bf16[512,1024]{1,0:T(8,128)(2,1)}, bf16[512,1024]{1,0:T(8,128)(2,1)S(1)}, u32[]{:S(2)}) copy-start(bf16[512,1024]{1,0:T(8,128)(2,1)S(1)} %get-tuple-element.12) | copy-start | bytes 3145732
  87.2 10.3 %copy-start.7 = (bf16[512,1024]{1,0:T(8,128)(2,1)}, bf16[512,1024]{1,0:T(8,128)(2,1)S(1)}, u32[]{:S(2)}) copy-start(bf16[512,1024]{1,0:T(8,128)(2,1)S(1)} %get-tuple-element.10) | copy-start | bytes 3145732
  87.3 10.2 %slice-start.5 = ((s8[6291456]{0:T(1024)(128)(4,1)}), s8[2097152]{0:T(1024)(128)(4,1)S(1)}, s32[]{:S(2)}) async-start(s8[6291456]{0:T(1024)(128)(4,1)} %bitcast.114), calls=%async_computation.12 | async-start | bytes 4194304
  241.6 6.4 %copy-start.4 = (s32[64,2]{0,1:T(2,128)S(1)}, s32[64,2]{0,1:T(2,128)}, u32[]{:S(2)}) copy-start(s32[64,2]{0,1:T(2,128)} %param.10) | copy-start | bytes 1540
  244.3 22.3 %all-to-all-start.3 = ((bf16[4,64,3072]{2,1,0:T(8,128)(2,1)}), bf16[4,64,3072]{2,1,0:T(8,128)(2,1)S(1)}, u32[]{:S(2)}, u32[]{:S(2)}) async-start(bf16[4,64,3072]{2,1,0:T(8,128)(2,1)} %bitcast.107), calls=%async_computation.3 | async-start | bytes 3145728 | tf_op jit(solution)/shard_map/all_to_all | solution.py:56
  248.1 8.6 %copy-start.2 = (bf16[2,256,3072]{2,1,0:T(8,128)(2,1)S(1)}, bf16[2,256,3072]{2,1,0:T(8,128)(2,1)}, u32[]{:S(2)}) copy-start(bf16[2,256,3072]{2,1,0:T(8,128)(2,1)} %get-tuple-element.6) | copy-start | bytes 9437188
  266.6 23.1 %all-to-all-start.1 = ((bf16[4,64,3072]{2,1,0:T(8,128)(2,1)}), bf16[4,64,3072]{2,1,0:T(8,128)(2,1)}, u32[]{:S(2)}, u32[]{:S(2)}) async-start(bf16[4,64,3072]{2,1,0:T(8,128)(2,1)} %bitcast.106), calls=%async_computation.1 | async-start | bytes 3145728 | tf_op jit(solution)/shard_map/all_to_all | solution.py:56
  270.9 8.5 %copy-start.6 = (bf16[8,64,3072]{2,1,0:T(8,128)(2,1)S(1)}, bf16[8,64,3072]{2,1,0:T(8,128)(2,1)}, u32[]{:S(2)}) copy-start(bf16[8,64,3072]{2,1,0:T(8,128)(2,1)} %all-gather.3.cloned.1.call-done) | copy-start | bytes 9437188
  270.9 8.5 %copy-start.8 = (bf16[512,1024]{1,0:T(8,128)(2,1)S(1)}, bf16[512,1024]{1,0:T(8,128)(2,1)}, u32[]{:S(2)}) copy-start(bf16[512,1024]{1,0:T(8,128)(2,1)} %copy-done.7) | copy-start | bytes 3145732
  284.8 7.2 %copy-start.3 = (f32[3072,4]{0,1:T(4,128)S(1)}, f32[3072,4]{0,1:T(4,128)}, u32[]{:S(2)}) copy-start(f32[3072,4]{0,1:T(4,128)} %param.9) | copy-start | bytes 147460
  289.7 2.4 copy-start.1
Sparse Core Ops, SparseCore 0:
  37.0 13.7 all-gather.4
  58.1 15.1 all-gather.2
  104.5 137.1 all-reduce.2
where the time goes:
time: 330 us
  waiting for transfers between devices  158 us (48%)
  blocking collectives  71 us (22%)
  matrix products  67.8 us (21%)
  between operations  14.1 us (4%)
  other arithmetic  9.3 us (3%)
  starting transfers between devices  8.22 us (2%)
    psum x1, waiting for transfers between devices, combine(): lax.psum(partial_value.reshape(dp_count, block_rows, features).astype(jnp...  137 us
    all_to_all x2, blocking collectives, spread(): lax.all_to_all(buffer, 'expert', split_axis=0, concat_axis=0, tiled=True)  43 us
    psum x1, blocking collectives, local(): lax.psum(router_term.astype(jnp.bfloat16), ('dp', 'expert'))  28 us
    all_to_all x2, waiting for transfers between devices, combine(): lax.all_to_all(own_rows, 'expert', split_axis=0, concat_axis=0, tiled=True)  11.9 us
    all_gather x2, waiting for transfers between devices, spread(): return lax.all_gather(arrived, 'dp', axis=0, tiled=True)  8.71 us
    dot_general x1, matrix products, local(): jnp.einsum('rf,rd->fd', hidden, cot_in, preferred_element_type=jnp.float32)  8.54 us
    dot_general x1, matrix products, local(): jnp.einsum('rd,rf->df', rows_in, up_grad, preferred_element_type=jnp.floa...  8.5 us
    all_to_all x2, starting transfers between devices, combine(): lax.all_to_all(own_rows, 'expert', split_axis=0, concat_axis=0, tiled=True)  8.1 us
  transfers between devices with their start and end apart: 5, of which 4 were waited for; matrix products, arithmetic and copies ran while one was open for 10% of the time, Pallas kernels for 0%

commit v1 on v0

--- a/solution.py
+++ b/solution.py
@@ -48,8 +48,12 @@
     pieces = 1
 
     def combine(partial_value):
-        summed = lax.psum(
-            partial_value.reshape(dp_count, block_rows, features).astype(jnp.bfloat16), ("dp", "mp")
+        summed = jnp.sum(
+            lax.all_gather(
+                partial_value.reshape(dp_count, block_rows, features).astype(jnp.bfloat16),
+                ("dp", "mp"),
+            ),
+            axis=0,
         ).astype(jnp.float32)
         own_rows = lax.dynamic_index_in_dim(summed, lax.axis_index("dp"), 0, keepdims=False)
         own_rows = own_rows.astype(jnp.bfloat16).reshape(exp_count, slot_count, features)

time: 330 us -> 657 us (1.99)
  waiting for transfers between devices: 158 us -> 454 us
  other arithmetic: 9.3 us -> 34.4 us
    all_gather x0 -> x2, waiting for transfers between devices: none -> 406 us  [combine(): lax.all_gather(partial_value.reshape(dp_count, block_rows, features).asty...]
    psum x1 -> x0, waiting for transfers between devices: 137 us -> none  [combine(): lax.psum(partial_value.reshape(dp_count, block_rows, features).astype(jnp...]
    reduce_sum x0 -> x2, other arithmetic: none -> 28.2 us  [combine(): jnp.sum(lax.all_gather(partial_value.reshape(dp_count, block_rows, featur...]
    all_gather x2, waiting for transfers between devices: 8.71 us -> 24.9 us  [spread(): return lax.all_gather(arrived, 'dp', axis=0, tiled=True)]
    all_to_all x2, waiting for transfers between devices: 11.9 us -> 23.3 us  [combine(): lax.all_to_all(own_rows, 'expert', split_axis=0, concat_axis=0, tiled=True)]
  transfers between devices with their start and end apart: 5 -> 6, of which waited for: 4 -> 6; matrix products, arithmetic and copies ran while one was open for 10% -> 4% of each run, Pallas kernels for 0% -> 0%
where the time goes in v1:
time: 657 us; the launch traced here: 655 us
  waiting for transfers between devices  454 us (69%)
  blocking collectives  71.6 us (11%)
  matrix products  70.4 us (11%)
  other arithmetic  34.4 us (5%)
  between operations  14 us (2%)
  starting transfers between devices  7.82 us (1%)
    all_gather x2, waiting for transfers between devices, combine(): lax.all_gather(partial_value.reshape(dp_count, block_rows, features).asty...  406 us
    all_to_all x2, blocking collectives, spread(): lax.all_to_all(buffer, 'expert', split_axis=0, concat_axis=0, tiled=True)  44.1 us
    reduce_sum x2, other arithmetic, combine(): jnp.sum(lax.all_gather(partial_value.reshape(dp_count, block_rows, featur...  28.2 us
    psum x1, blocking collectives, local(): lax.psum(router_term.astype(jnp.bfloat16), ('dp', 'expert'))  27.5 us
    all_gather x2, waiting for transfers between devices, spread(): return lax.all_gather(arrived, 'dp', axis=0, tiled=True)  24.9 us
    all_to_all x2, waiting for transfers between devices, combine(): lax.all_to_all(own_rows, 'expert', split_axis=0, concat_axis=0, tiled=True)  23.3 us
  transfers between devices with their start and end apart: 6, of which 6 were waited for; matrix products, arithmetic and copies ran while one was open for 4% of the time, Pallas kernels for 0%

profile of v1, /device:TPU:1, one launch (start us, length us, event | category | flops | bytes accessed | tf_op | source)
XLA Modules:
  0.0 654.8 jit_solution(16385268863489094375)
XLA Ops:
  11.0 22.7 %all_to_all.20 = bf16[4,64,3072]{2,1,0:T(8,128)(2,1)} all-to-all(bf16[4,64,3072]{2,1,0:T(8,128)(2,1)S(1)} %bitcast.136), channel_id=1, replica_groups=mesh['dp'=2,'expert'=4,'mp'=4] {'expert'}, dimensions={0} | all-to-all | bytes 3145728 | tf_op jit(solution)/shard_map/all_to_all | solution.py:44
  33.7 13.9 %all-gather.7.cloned.1.call-done = bf16[8,64,3072]{2,1,0:T(8,128)(2,1)} async-done(((bf16[4,64,3072]{2,1,0:T(8,128)(2,1)}), bf16[8,64,3072]{2,1,0:T(8,128)(2,1)}) %all-gather.7.cloned.1.call-update) | async-done | bytes 3145744 | tf_op jit(solution)/shard_map/all_gather | solution.py:45
  47.6 7.4 %fusion.10 = f32[512,1024]{1,0:T(8,128)S(1)} fusion(bf16[512,3072]{1,0:T(8,128)(2,1)} %bitcast.143, bf16[1,3072,1024]{2,1,0:T(8,128)(2,1)} %param.12), kind=kOutput, calls=%fused_computation.12 | convolution fusion | flops 3221225472 | bytes 11534336 | tf_op jit(solution)/shard_map/dot_general | solution.py:66
  55.1 8.3 %multiply_convert_fusion.2 = (bf16[512,1024]{1,0:T(8,128)(2,1)S(1)}, f32[512,1024]{1,0:T(8,128)}) fusion(f32[512,1024]{1,0:T(8,128)S(1)} %fusion.10, bf16[512,3072]{1,0:T(8,128)(2,1)S(1)} %bitcast.146, bf16[1,3072,1024]{2,1,0:T(8,128)(2,1)} %param.13), kind=kOutput, calls=%fused_computation.33 | convolution fusion | flops 3224371200 | bytes 14680064 | tf_op jit(solution)/shard_map/dot_general | solution.py:67
  63.4 4.8 fusion.17
  68.2 221.2 %all-gather.11.cloned.1.call-done = bf16[16,1,256,3072]{3,2,1,0:T(8,128)(2,1)} async-done(((bf16[2,1,256,3072]{3,2,1,0:T(8,128)(2,1)}), bf16[16,1,256,3072]{3,2,1,0:T(8,128)(2,1)}) %all-gather.11.cloned.1.call-update) | async-done | bytes 25165840 | tf_op jit(solution)/shard_map/all_gather | solution.py:52
  289.5 14.1 %bitcast_reduce_fusion.1 = bf16[2,256,3072]{2,1,0:T(8,128)(2,1)S(1)} fusion(bf16[8,2,256,3072]{3,2,1,0:T(8,128)(2,1)} %bitcast.132), kind=kLoop, calls=%fused_computation.1 | loop fusion | flops 11010048 | bytes 28311552 | tf_op jit(solution)/shard_map/reduce_sum | solution.py:51
  304.8 3.7 all-to-all-start.1
  309.1 18.4 %all-to-all-done.1 = bf16[4,64,3072]{2,1,0:T(8,128)(2,1)S(1)} async-done(((bf16[4,64,3072]{2,1,0:T(8,128)(2,1)}), bf16[4,64,3072]{2,1,0:T(8,128)(2,1)S(1)}, u32[]{:S(2)}, u32[]{:S(2)}) %all-to-all-start.1) | async-done | bytes 1572896 | tf_op jit(solution)/shard_map/all_to_all | solution.py:60
  328.7 1.9 multiply_reduce_fusion
  331.3 21.4 %all_to_all.21 = bf16[4,64,3072]{2,1,0:T(8,128)(2,1)} all-to-all(bf16[4,64,3072]{2,1,0:T(8,128)(2,1)S(1)} %bitcast.139), channel_id=1, replica_groups=mesh['dp'=2,'expert'=4,'mp'=4] {'expert'}, dimensions={0} | all-to-all | bytes 3145728 | tf_op jit(solution)/shard_map/all_to_all | solution.py:44
  353.0 11.0 %all-gather.9.cloned.1.call-done = bf16[8,64,3072]{2,1,0:T(8,128)(2,1)} async-done(((bf16[4,64,3072]{2,1,0:T(8,128)(2,1)}), bf16[8,64,3072]{2,1,0:T(8,128)(2,1)}) %all-gather.9.cloned.1.call-update) | async-done | bytes 3145744 | tf_op jit(solution)/shard_map/all_gather | solution.py:45
  364.0 8.9 %multiply_convert_fusion.1 = (bf16[512,1024]{1,0:T(8,128)(2,1)S(1)}, bf16[512,1024]{1,0:T(8,128)(2,1)S(1)}) fusion(f32[512,1024]{1,0:T(8,128)} %copy-done.13, f32[512,1024]{1,0:T(8,128)} %get-tuple-element.13, bf16[512,3072]{1,0:T(8,128)(2,1)} %bitcast.147, bf16[1,1024,3072]{2,1,0:T(8,128)(2,1)} %param.14), kind=kOutput, calls=%fused_computation.32 | convolution fusion | flops 3228041216 | bytes 15728640 | tf_op jit(solution)/shard_map/rd,fd->rf/dot_general | solution.py:93
  372.9 6.3 fusion
  379.3 7.7 %fusion.20 = bf16[2,1,256,3072]{3,2,1,0:T(8,128)(2,1)} fusion(f32[2,256,3072]{2,1,0:T(8,128)S(1)} %fusion, bf16[2,256,1024]{2,1,0:T(8,128)(2,1)S(1)} %bitcast.151, bf16[1,3072,1024]{2,1,0:T(8,128)(2,1)} %param.12), kind=kOutput, calls=%fused_computation.20 | convolution fusion | flops 3224371200 | bytes 16777216 | tf_op jit(solution)/shard_map/prf,qdf->pqrd/dot_general | solution.py:109
  387.3 27.5 %psum.7 = bf16[3072,4]{0,1:T(4,128)(2,1)S(1)} all-reduce(bf16[3072,4]{0,1:T(4,128)(2,1)S(1)} %fusion.26), channel_id=1, replica_groups=mesh['dp'=2,'expert'=4,'mp'=4] {'dp','expert'}, use_global_device_ids=true, to_apply=%region_8.9 | all-reduce | flops 12288 | bytes 49152 | tf_op jit(solution)/shard_map/psum | solution.py:90
  416.4 7.2 %convert_bitcast_fusion.2 = bf16[1,3072,1024]{2,1,0:T(8,128)(2,1)} fusion(bf16[512,3072]{1,0:T(8,128)(2,1)} %bitcast.144, bf16[512,1024]{1,0:T(8,128)(2,1)S(1)} %copy-done.12), kind=kOutput, calls=%fused_computation.16 | convolution fusion | flops 3224371200 | bytes 10485760 | tf_op jit(solution)/shard_map/rd,rf->df/dot_general | solution.py:101
  423.6 184.6 %all-gather.13.cloned.1.call-done = bf16[16,1,256,3072]{3,2,1,0:T(8,128)(2,1)} async-done(((bf16[2,1,256,3072]{3,2,1,0:T(8,128)(2,1)}), bf16[16,1,256,3072]{3,2,1,0:T(8,128)(2,1)}) %all-gather.13.cloned.1.call-update) | async-done | bytes 25165840 | tf_op jit(solution)/shard_map/all_gather | solution.py:52
  608.3 14.1 %bitcast_reduce_fusion = bf16[2,256,3072]{2,1,0:T(8,128)(2,1)S(1)} fusion(bf16[8,2,256,3072]{3,2,1,0:T(8,128)(2,1)} %bitcast.133), kind=kLoop, calls=%fused_computation | loop fusion | flops 11010048 | bytes 28311552 | tf_op jit(solution)/shard_map/reduce_sum | solution.py:51
  623.7 3.8 all-to-all-start.3
  627.5 8.5 %convert_bitcast_fusion.1 = bf16[1,3072,1024]{2,1,0:T(8,128)(2,1)} fusion(bf16[512,3072]{1,0:T(8,128)(2,1)} %bitcast.145, bf16[512,1024]{1,0:T(8,128)(2,1)} %copy-done.10), kind=kOutput, calls=%fused_computation.15 | convolution fusion | flops 3224371200 | bytes 10485760 | tf_op jit(solution)/shard_map/rd,rf->df/dot_general | solution.py:104
  636.0 5.4 convert_bitcast_fusion
  641.3 4.9 all-to-all-done.3
  646.6 1.6 fusion.25
  (66 shorter events, 11.3 us)
Async XLA Ops:
  7.2 3.2 copy-start
  7.2 40.4 %all-gather.7.cloned.1.call-start = ((), (), s32[]{:S(2)}) async-start(), calls=%async_computation.4 | async-start | bytes 4718592 | tf_op jit(solution)/shard_map/all_gather | solution.py:45
  33.7 29.7 %slice-start = ((s8[6291456]{0:T(1024)(128)(4,1)}), s8[2097152]{0:T(1024)(128)(4,1)S(1)}, s32[]{:S(2)}) async-start(s8[6291456]{0:T(1024)(128)(4,1)} %bitcast.141), calls=%async_computation.8 | async-start | bytes 4194304
  33.7 255.8 %all-gather.11.cloned.1.call-start = ((), (), s32[]{:S(2)}) async-start(), calls=%async_computation.6 | async-start | bytes 28311552 | tf_op jit(solution)/shard_map/all_gather | solution.py:52
  47.6 7.4 %copy-start.6 = (bf16[8,64,3072]{2,1,0:T(8,128)(2,1)S(1)}, bf16[8,64,3072]{2,1,0:T(8,128)(2,1)}, u32[]{:S(2)}) copy-start(bf16[8,64,3072]{2,1,0:T(8,128)(2,1)} %all-gather.7.cloned.1.call-done) | copy-start | bytes 9437188
  47.6 15.8 %slice-start.1 = ((s8[6291456]{0:T(1024)(128)(4,1)}), s8[4194304]{0:T(1024)(128)(4,1)S(1)}, s32[]{:S(2)}) async-start(s8[6291456]{0:T(1024)(128)(4,1)} %bitcast.141), calls=%async_computation.9 | async-start | bytes 8388608
  55.0 8.3 %copy-start.13 = (f32[512,1024]{1,0:T(8,128)}, f32[512,1024]{1,0:T(8,128)S(1)}, u32[]{:S(2)}) copy-start(f32[512,1024]{1,0:T(8,128)S(1)} %fusion.10) | copy-start | bytes 6291460
  63.4 4.8 copy-start.8
  304.8 3.8 copy-start.2
  304.8 3.8 copy-start.3
  304.8 4.2 copy-start.5
  304.8 22.7 %all-to-all-start.1 = ((bf16[4,64,3072]{2,1,0:T(8,128)(2,1)}), bf16[4,64,3072]{2,1,0:T(8,128)(2,1)S(1)}, u32[]{:S(2)}, u32[]{:S(2)}) async-start(bf16[4,64,3072]{2,1,0:T(8,128)(2,1)} %bitcast.138), calls=%async_computation.1 | async-start | bytes 3145728 | tf_op jit(solution)/shard_map/all_to_all | solution.py:60
  308.5 55.5 %all-gather.9.cloned.1.call-start = ((), (), s32[]{:S(2)}) async-start(), calls=%async_computation.5 | async-start | bytes 4718592 | tf_op jit(solution)/shard_map/all_gather | solution.py:45
  327.5 1.1 copy-start.1
  352.8 255.5 %all-gather.13.cloned.1.call-start = ((), (), s32[]{:S(2)}) async-start(), calls=%async_computation.7 | async-start | bytes 28311552 | tf_op jit(solution)/shard_map/all_gather | solution.py:52
  372.9 6.4 copy-start.10
  372.9 6.4 copy-start.11
  387.0 29.4 %copy-start.12 = (bf16[512,1024]{1,0:T(8,128)(2,1)S(1)}, bf16[512,1024]{1,0:T(8,128)(2,1)}, u32[]{:S(2)}) copy-start(bf16[512,1024]{1,0:T(8,128)(2,1)} %copy-done.11) | copy-start | bytes 3145732
  623.7 22.5 %all-to-all-start.3 = ((bf16[4,64,3072]{2,1,0:T(8,128)(2,1)}), bf16[4,64,3072]{2,1,0:T(8,128)(2,1)S(1)}, u32[]{:S(2)}, u32[]{:S(2)}) async-start(bf16[4,64,3072]{2,1,0:T(8,128)(2,1)} %bitcast.137), calls=%async_computation.3 | async-start | bytes 3145728 | tf_op jit(solution)/shard_map/all_to_all | solution.py:60
  627.5 8.5 %copy-start.7 = (bf16[8,64,3072]{2,1,0:T(8,128)(2,1)S(1)}, bf16[8,64,3072]{2,1,0:T(8,128)(2,1)}, u32[]{:S(2)}) copy-start(bf16[8,64,3072]{2,1,0:T(8,128)(2,1)} %all-gather.9.cloned.1.call-done) | copy-start | bytes 9437188
  627.5 8.5 %copy-start.9 = (bf16[512,1024]{1,0:T(8,128)(2,1)S(1)}, bf16[512,1024]{1,0:T(8,128)(2,1)}, u32[]{:S(2)}) copy-start(bf16[512,1024]{1,0:T(8,128)(2,1)} %copy-done.8) | copy-start | bytes 3145732
  641.3 5.3 copy-start.4
Sparse Core Ops, SparseCore 0:
  33.8 13.7 all-gather.6
  68.3 221.0 all-gather.10
  352.9 11.0 all-gather.8
  387.1 221.0 all-gather.12
